TPU v7x, 32 devices: a whole 2x2x4 slice. The times are simulated.
32 devices in a mesh: row: 4 (over z), col: 8 (over y, x, core).
Axes of the slice: x: 2, y: 2, z: 4, core: 2. Of those that a mesh axis runs over, the one named last changes fastest.
Arguments:
- matrix: float32 [6144, 6144], P('row', 'col'), may hold values from -160 to 160, as said below
- pattern: int32 [16, 16], replicated, may hold values from 0 to 1, as said below
- row_order: int32 [16], replicated, may hold values from 0 to 15, as said below
- col_order: int32 [16], replicated, may hold values from 0 to 15, as said below
Outputs:
- factored: float32 [6144, 6144], P('row', 'col')
Inputs may be any that keep to these rules, and one draw needn't show every extreme that they name: `row_order`: a permutation of 0 to 15. `col_order`: a permutation of 0 to 15. Symmetric with ones on the diagonal; pattern[1, 0] = 1; pattern[I, J] = 1 whenever pattern[I, 0] = pattern[J, 0] = 1, and whenever pattern[I, 1] = pattern[J, 1] = 1 with I, J >= 1. `matrix`: read in natural block order the window is symmetric, and its retained lower blocks make the pivot block of supernode 0, and that of supernode 1 after the first update, positive definite.
All inputs are finite; a program needn't handle non-finite values.
Results may differ from a plain program's by a relative error of at most 0.0003.
Values sent between devices are 32-bit elements; how exact they have to be, the bound alone decides.
No kernel may reach another device: no remote copies, remote signals or barrier semaphores. Data moves between devices by JAX's collectives and lax.ppermute only.
A program may use at most 128 MiB of HBM per device.

v0:
```python
import jax
import jax.numpy as jnp
from jax import lax
from jax.sharding import PartitionSpec as P

BLOCK = 384


def spread(value, axis, root):
    mine = lax.axis_index(axis) == root
    return lax.psum(jnp.where(mine, value, jnp.zeros_like(value)), axis)


def positions(order):
    indices = jnp.arange(order.shape[0], dtype=jnp.int32)
    return jnp.sum(jnp.where(order[None, :] == indices[:, None], indices[None, :], 0), axis=1)


def look_up(table, wanted):
    indices = jnp.arange(table.shape[0], dtype=jnp.int32)
    return jnp.sum(jnp.where(indices[None, :] == wanted[:, None], table[None, :], 0), axis=1)


def expand(flags, tall, broad):
    return jnp.repeat(jnp.repeat(flags, tall, axis=0), broad, axis=1)


def body(matrix, pattern, row_order, col_order):
    local_rows, width = matrix.shape
    total = row_order.shape[0]
    blocks_here = local_rows // BLOCK
    piece_width = min(width, BLOCK)
    piece_count = width // piece_width
    row_here = lax.axis_index("row")
    col_here = lax.axis_index("col")
    row_place = positions(row_order)
    col_place = positions(col_order)
    indices = jnp.arange(total, dtype=jnp.int32)
    stored_rows = row_here * blocks_here + jnp.arange(blocks_here, dtype=jnp.int32)
    row_ids = look_up(row_order, stored_rows)
    starts = col_here * width + piece_width * jnp.arange(piece_count, dtype=jnp.int32)
    col_ids = look_up(col_order, starts // BLOCK)
    offsets = starts % BLOCK
    row_select = (row_ids[:, None] == indices[None, :]).astype(jnp.int32)
    col_select = (col_ids[:, None] == indices[None, :]).astype(jnp.int32)
    marked = jnp.dot(jnp.dot(row_select, pattern), col_select.T)
    lower = row_ids[:, None] >= col_ids[None, :]
    retain = expand((marked == 1) & lower, BLOCK, piece_width).astype(jnp.float32)
    lower_full = expand(lower, BLOCK, piece_width).astype(jnp.float32)
    current = matrix * retain
    identity = jnp.eye(BLOCK, dtype=jnp.float32)
    for supernode in range(2):
        wanted = jnp.full((1,), supernode, jnp.int32)
        center = look_up(row_place, wanted)[0]
        root_row = center // blocks_here
        center_local = center % blocks_here
        column_start = look_up(col_place, wanted)[0] * BLOCK
        in_column = look_up(pattern[:, supernode], row_ids)
        struct_rows = ((in_column == 1) & (row_ids > supernode)).astype(jnp.float32)
        used_rows = jnp.repeat(struct_rows, BLOCK)
        anchor = column_start + 0
        section = lax.dynamic_slice_in_dim(current, anchor % width, piece_width, 1)
        received = spread(section, "col", anchor // width)
        center_rows = lax.dynamic_slice_in_dim(received, center_local * BLOCK, BLOCK, 0)
        pivot_values = spread(center_rows, "row", root_row)
        factor = jnp.linalg.cholesky(pivot_values)
        inverse = jax.scipy.linalg.solve_triangular(factor, identity, lower=True)
        scaled = jnp.dot(received * used_rows[:, None], inverse.T, precision=lax.Precision.HIGHEST)
        fetched = []
        for column_piece in range(piece_count):
            holder = look_up(row_place, col_ids[column_piece : column_piece + 1])[0]
            section = lax.dynamic_slice_in_dim(
                scaled, holder % blocks_here * BLOCK + offsets[column_piece], piece_width, 0
            )
            fetched.append(spread(section, "row", holder // blocks_here))
        across = jnp.concatenate(fetched, axis=0)
        update = jnp.dot(scaled, across.T, precision=lax.Precision.HIGHEST)
        current = current - update * lower_full
        is_center = jnp.repeat(row_ids == supernode, BLOCK)
        column = jnp.where(is_center[:, None], jnp.tile(factor, (blocks_here, 1)), scaled)
        replaced = []
        for column_piece in range(piece_count):
            present = lax.dynamic_slice_in_dim(current, column_piece * piece_width, piece_width, 1)
            replaced.append(jnp.where(col_ids[column_piece] == supernode, column, present))
        current = jnp.concatenate(replaced, axis=1)
    return current * retain


def solution(mesh):
    in_specs = (P("row", "col"), P(), P(), P())
    out_specs = P("row", "col")
    return jax.shard_map(body, mesh=mesh, in_specs=in_specs, out_specs=out_specs, check_vma=False)
```

profile of v0, /device:TPU:0, one launch (start us, length us, event | category | flops | bytes accessed | tf_op | source)
XLA Modules:
  0.0 607.0 jit_solution(9962153152874555031)
XLA Ops:
  9.5 2.0 fusion.84
  14.1 6.0 copy.17
  20.2 2.9 bitcast_select_fusion.3
  23.1 2.2 copy-done
  25.2 1.7 dynamic-slice_select_fusion
  29.5 63.3 %all-reduce.10.cloned.1.call-done = f32[1536,384]{0,1:T(8,128)} async-done(((f32[1536,384]{0,1:T(8,128)}), f32[1536,384]{0,1:T(8,128)}) %all-reduce.10.cloned.1.call-update) | async-done | bytes 2359312 | tf_op jit(solution)/shard_map/psum | solution.py:11
  92.8 1.9 dynamic-slice_select_fusion.6
  103.5 30.7 %all-reduce.12.cloned.1.call-done = f32[384,384]{0,1:T(8,128)} async-done(((f32[384,384]{0,1:T(8,128)}), f32[384,384]{0,1:T(8,128)}) %all-reduce.12.cloned.1.call-update) | async-done | bytes 589840 | tf_op jit(solution)/shard_map/psum | solution.py:11
  134.2 1.3 copy.18
  136.7 11.7 %cholesky.208 = f32[128,128]{1,0:T(8,128)S(1)} custom-call(f32[128,128]{1,0:T(8,128)S(1)} %cholesky.310), custom_call_target="Cholesky" | custom-call | tf_op jit(solution)/shard_map/jit(cholesky)/cholesky | solution.py:66
  148.5 9.8 %custom-call.20 = f32[1,128,128]{1,2,0:T(8,128)S(1)} custom-call(f32[1,128,128]{2,1,0:T(8,128)S(1)} %get-tuple-element.82), custom_call_target="InvertDiagBlocksLowerTriangular" | custom-call | tf_op jit(solution)/shard_map/jit(cholesky)/cholesky | solution.py:66
  158.9 11.7 %cholesky.227 = f32[128,128]{1,0:T(8,128)S(1)} custom-call(f32[128,128]{1,0:T(8,128)S(1)} %cholesky.314), custom_call_target="Cholesky" | custom-call | tf_op jit(solution)/shard_map/jit(cholesky)/cholesky | solution.py:66
  171.9 10.1 %custom-call.21 = f32[1,128,128]{1,2,0:T(8,128)S(1)} custom-call(f32[1,128,128]{2,1,0:T(8,128)S(1)} %get-tuple-element.79), custom_call_target="InvertDiagBlocksLowerTriangular" | custom-call | tf_op jit(solution)/shard_map/jit(cholesky)/cholesky | solution.py:66
  182.5 11.7 %cholesky.246 = f32[128,128]{1,0:T(8,128)S(1)} custom-call(f32[128,128]{1,0:T(8,128)S(1)} %convolution_subtract_fusion.7), custom_call_target="Cholesky" | custom-call | tf_op jit(solution)/shard_map/jit(cholesky)/cholesky | solution.py:66
  196.8 5.6 while.4
  197.4 1.3 bitcast_dynamic-update-slice_fusion.4
  199.3 1.3 bitcast_dynamic-update-slice_fusion.4
  201.2 1.3 bitcast_dynamic-update-slice_fusion.4
  202.4 29.5 %custom-call.22 = f32[3,128,128]{1,2,0:T(8,128)S(1)} custom-call(f32[3,128,128]{2,1,0:T(8,128)S(1)} %get-tuple-element.21), custom_call_target="InvertDiagBlocksLowerTriangular" | custom-call | tf_op jit(solution)/shard_map/jit(_solve_triangular)/triangular_solve | solution.py:67
  233.8 5.7 fusion.6
  239.5 1.4 dynamic-slice_select_fusion.5
  244.1 1.3 broadcast_in_dim.166
  247.2 1.5 tile.8
  248.6 1.6 copy.24
  250.2 46.4 %all-reduce.20.cloned.1.call-done = (f32[384,384]{0,1:T(8,128)}, f32[384,384]{0,1:T(8,128)}) async-done(((f32[384,384]{0,1:T(8,128)}, f32[384,384]{0,1:T(8,128)}), (f32[384,384]{0,1:T(8,128)}, f32[384,384]{0,1:T(8,128)})) %all-reduce.20.cloned.1.call-update) | async-done | bytes 1179664 | tf_op jit(solution)/shard_map/psum | solution.py:11
  296.6 10.6 %fusion.1 = f32[1536,768]{0,1:T(8,128)S(1)} fusion(f32[1536,768]{0,1:T(8,128)} %copy-done, f32[1536,384]{0,1:T(8,128)S(1)} %fusion.6, pred[1536,2]{0,1:T(4,128)(4,1)S(1)} %bitcast.119, f32[384,384]{0,1:T(8,128)} %get-tuple-element.51, f32[384,384]{0,1:T(8,128)} %get-tuple-element.52), kind=kOutput, calls=%fused_computation.12 | convolution fusion | flops 5438472192 | bytes 12979200 | tf_op jit(solution)/shard_map/dot_general | solution.py:77
  308.3 1.4 copy-done.1
  310.5 2.6 fusion.3
  315.9 59.7 %all-reduce.14.cloned.1.call-done = f32[1536,384]{0,1:T(8,128)} async-done(((f32[1536,384]{0,1:T(8,128)}), f32[1536,384]{0,1:T(8,128)}) %all-reduce.14.cloned.1.call-update) | async-done | bytes 2359312 | tf_op jit(solution)/shard_map/psum | solution.py:11
  375.6 1.9 dynamic-slice_select_fusion.3
  378.5 38.4 %all-reduce.16.cloned.1.call-done = f32[384,384]{0,1:T(8,128)} async-done(((f32[384,384]{0,1:T(8,128)}), f32[384,384]{0,1:T(8,128)}) %all-reduce.16.cloned.1.call-update) | async-done | bytes 589840 | tf_op jit(solution)/shard_map/psum | solution.py:11
  416.9 1.3 copy.20
  419.3 11.7 %cholesky.261 = f32[128,128]{1,0:T(8,128)S(1)} custom-call(f32[128,128]{1,0:T(8,128)S(1)} %cholesky.318), custom_call_target="Cholesky" | custom-call | tf_op jit(solution)/shard_map/jit(cholesky)/cholesky | solution.py:66
  431.1 9.8 %custom-call.23 = f32[1,128,128]{1,2,0:T(8,128)S(1)} custom-call(f32[1,128,128]{2,1,0:T(8,128)S(1)} %get-tuple-element.75), custom_call_target="InvertDiagBlocksLowerTriangular" | custom-call | tf_op jit(solution)/shard_map/jit(cholesky)/cholesky | solution.py:66
  441.5 11.7 %cholesky.280 = f32[128,128]{1,0:T(8,128)S(1)} custom-call(f32[128,128]{1,0:T(8,128)S(1)} %cholesky.322), custom_call_target="Cholesky" | custom-call | tf_op jit(solution)/shard_map/jit(cholesky)/cholesky | solution.py:66
  454.5 10.0 %custom-call.24 = f32[1,128,128]{1,2,0:T(8,128)S(1)} custom-call(f32[1,128,128]{2,1,0:T(8,128)S(1)} %get-tuple-element.72), custom_call_target="InvertDiagBlocksLowerTriangular" | custom-call | tf_op jit(solution)/shard_map/jit(cholesky)/cholesky | solution.py:66
  465.0 11.7 %cholesky.299 = f32[128,128]{1,0:T(8,128)S(1)} custom-call(f32[128,128]{1,0:T(8,128)S(1)} %convolution_subtract_fusion.6), custom_call_target="Cholesky" | custom-call | tf_op jit(solution)/shard_map/jit(cholesky)/cholesky | solution.py:66
  479.3 5.6 while.5
  480.0 1.2 bitcast_dynamic-update-slice_fusion.5
  483.7 1.2 bitcast_dynamic-update-slice_fusion.5
  485.0 29.5 %custom-call.25 = f32[3,128,128]{1,2,0:T(8,128)S(1)} custom-call(f32[3,128,128]{2,1,0:T(8,128)S(1)} %get-tuple-element.22), custom_call_target="InvertDiagBlocksLowerTriangular" | custom-call | tf_op jit(solution)/shard_map/jit(_solve_triangular)/triangular_solve | solution.py:67
  516.3 5.7 fusion.4
  522.0 1.4 dynamic-slice_select_fusion.2
  525.3 1.5 copy.26
  526.9 52.2 %all-reduce.18.cloned.1.call-done = (f32[384,384]{0,1:T(8,128)}, f32[384,384]{0,1:T(8,128)}) async-done(((f32[384,384]{0,1:T(8,128)}, f32[384,384]{0,1:T(8,128)}), (f32[384,384]{0,1:T(8,128)}, f32[384,384]{0,1:T(8,128)})) %all-reduce.18.cloned.1.call-update) | async-done | bytes 1179664 | tf_op jit(solution)/shard_map/psum | solution.py:11
  579.1 10.9 %fusion = f32[1536,768]{0,1:T(8,128)S(1)} fusion(f32[1536,384]{0,1:T(8,128)} %copy-done.2, f32[1536,384]{0,1:T(8,128)} %copy-done.1, f32[1536,384]{0,1:T(8,128)S(1)} %fusion.4, pred[1536,2]{0,1:T(4,128)(4,1)S(1)} %bitcast.120, f32[384,384]{0,1:T(8,128)} %get-tuple-element.49, f32[384,384]{0,1:T(8,128)} %get-tuple-element.50), kind=kOutput, calls=%fused_computation.11 | convolution fusion | flops 5439651840 | bytes 12979200 | tf_op jit(solution)/shard_map/dot_general | solution.py:77
  591.0 2.6 bitcast_select_fusion.2
  593.7 6.0 copy.22
  (120 shorter events, 32.2 us)
Async XLA Ops:
  6.5 86.3 %all-reduce.10.cloned.1.call-start = ((), (), s32[]{:S(2)}) async-start(), calls=%async_computation | async-start | bytes 4718592 | tf_op jit(solution)/shard_map/psum | solution.py:11
  8.2 12.0 %copy-start.9 = (s32[2]{0:T(128)}, s32[2]{0:T(128)S(1)}, u32[]{:S(2)}) copy-start(s32[2]{0:T(128)S(1)} %fusion.80) | copy-start | bytes 28
  23.1 2.2 copy-start
  27.0 2.4 copy-start.7
  27.0 107.2 %all-reduce.12.cloned.1.call-start = ((), (), s32[]{:S(2)}) async-start(), calls=%async_computation.1 | async-start | bytes 1179648 | tf_op jit(solution)/shard_map/psum | solution.py:11
  94.8 201.8 %all-reduce.20.cloned.1.call-start = ((), (), s32[]{:S(2)}) async-start(), calls=%async_computation.5 | async-start | bytes 2359296 | tf_op jit(solution)/shard_map/psum | solution.py:11
  240.9 134.8 %all-reduce.14.cloned.1.call-start = ((), (), s32[]{:S(2)}) async-start(), calls=%async_computation.2 | async-start | bytes 4718592 | tf_op jit(solution)/shard_map/psum | solution.py:11
  248.6 47.9 %copy-start.5 = (pred[1,2,4,384]{3,1,2,0:T(4,128)(4,1)S(1)}, pred[1,2,4,384]{3,1,2,0:T(4,128)(4,1)}, u32[]{:S(2)}) copy-start(pred[1,2,4,384]{3,1,2,0:T(4,128)(4,1)} %copy.25) | copy-start | bytes 9220
  296.6 10.7 %copy-start.4 = (f32[48,8,4,384]{3,1,2,0:T(8,128)S(1)}, f32[48,8,4,384]{3,1,2,0:T(8,128)}, u32[]{:S(2)}) copy-start(f32[48,8,4,384]{3,1,2,0:T(8,128)} %copy.24) | copy-start | bytes 7077892
  308.3 1.4 copy-start.1
  308.3 2.2 copy-start.2
  313.1 64.8 %copy-start.10 = (f32[4]{0:T(128)S(1)}, f32[4]{0:T(128)}, u32[]{:S(2)}) copy-start(f32[4]{0:T(128)} %get-tuple-element.84) | copy-start | bytes 52
  313.1 103.8 %all-reduce.16.cloned.1.call-start = ((), (), s32[]{:S(2)}) async-start(), calls=%async_computation.3 | async-start | bytes 1179648 | tf_op jit(solution)/shard_map/psum | solution.py:11
  377.6 201.5 %all-reduce.18.cloned.1.call-start = ((), (), s32[]{:S(2)}) async-start(), calls=%async_computation.4 | async-start | bytes 2359296 | tf_op jit(solution)/shard_map/psum | solution.py:11
  522.0 2.6 copy-start.8
  525.3 53.7 %copy-start.6 = (pred[1,2,4,384]{3,1,2,0:T(4,128)(4,1)S(1)}, pred[1,2,4,384]{3,1,2,0:T(4,128)(4,1)}, u32[]{:S(2)}) copy-start(pred[1,2,4,384]{3,1,2,0:T(4,128)(4,1)} %copy.25) | copy-start | bytes 9220
  579.1 10.9 %copy-start.3 = (f32[48,8,4,384]{3,1,2,0:T(8,128)S(1)}, f32[48,8,4,384]{3,1,2,0:T(8,128)}, u32[]{:S(2)}) copy-start(f32[48,8,4,384]{3,1,2,0:T(8,128)} %copy.26) | copy-start | bytes 7077892
Sparse Core Ops, SparseCore 0:
  27.1 65.6 all-reduce.9
  95.2 38.9 all-reduce.11
  241.0 55.5 all-reduce.19
  313.2 62.3 all-reduce.13
  377.8 38.9 all-reduce.15
  523.5 55.4 all-reduce.17
where the time goes:
time: 618 us; the launch traced here: 607 us
  waiting for transfers between devices  291 us (47%)
  other arithmetic  201 us (33%)
  local copies, waits for them, and re-layouts  42.1 us (7%)
  matrix products  39.5 us (6%)
  between operations  33.4 us (5%)
    psum x6, waiting for transfers between devices, spread(): return lax.psum(jnp.where(mine, value, jnp.zeros_like(value)), axis)  291 us
    another operation x22, other arithmetic, body(): factor = jnp.linalg.cholesky(pivot_values)  114 us
    another operation x5, other arithmetic, body(): inverse = jax.scipy.linalg.solve_triangular(factor, identity, lower=True)  59.1 us
    dot_general x2, matrix products, body(): update = jnp.dot(scaled, across.T, precision=lax.Precision.HIGHEST)  21.5 us
    unnamed x29, local copies, waits for them, and re-layouts  14.3 us
  transfers between devices with their start and end apart: 6, of which 6 were waited for; matrix products, arithmetic and copies ran while one was open for 2% of the time, Pallas kernels for 0%

commit v1 on v0

--- a/solution.py
+++ b/solution.py
@@ -8,7 +8,7 @@
 
 def spread(value, axis, root):
     mine = lax.axis_index(axis) == root
-    return lax.psum(jnp.where(mine, value, jnp.zeros_like(value)), axis)
+    return jnp.sum(lax.all_gather(jnp.where(mine, value, jnp.zeros_like(value)), axis), axis=0)
 
 
 def positions(order):

time: 618 us -> 863 us (1.40)
  waiting for transfers between devices: 291 us -> 456 us
  local copies, waits for them, and re-layouts: 42.1 us -> 104 us
  other arithmetic: 201 us -> 223 us
    all_gather x0 -> x8, waiting for transfers between devices: none -> 455 us  [spread(): lax.all_gather(jnp.where(mine, value, jnp.zeros_like(value)), axis)]
    psum x6 -> x0, waiting for transfers between devices: 291 us -> none  [spread(): return lax.psum(jnp.where(mine, value, jnp.zeros_like(value)), axis)]
    unnamed x29 -> x33, local copies, waits for them, and re-layouts: 14.3 us -> 56.8 us
    reduce_sum x0 -> x8, other arithmetic: none -> 25.5 us  [spread(): jnp.sum(lax.all_gather(jnp.where(mine, value, jnp.zeros_like(value)), axi...]
    all_gather x0 -> x6, local copies, waits for them, and re-layouts: none -> 20.4 us  [spread(): lax.all_gather(jnp.where(mine, value, jnp.zeros_like(value)), axis)]
  transfers between devices with their start and end apart: 6 -> 8, of which waited for: 6 -> 8; matrix products, arithmetic and copies ran while one was open for 2% -> 3% of each run, Pallas kernels for 0% -> 0%
where the time goes in v1:
time: 863 us; the launch traced here: 855 us
  waiting for transfers between devices  456 us (53%)
  other arithmetic  223 us (26%)
  local copies, waits for them, and re-layouts  104 us (12%)
  matrix products  39 us (5%)
  between operations  33 us (4%)
    all_gather x8, waiting for transfers between devices, spread(): lax.all_gather(jnp.where(mine, value, jnp.zeros_like(value)), axis)  455 us
    another operation x22, other arithmetic, body(): factor = jnp.linalg.cholesky(pivot_values)  114 us
    another operation x5, other arithmetic, body(): inverse = jax.scipy.linalg.solve_triangular(factor, identity, lower=True)  59.7 us
    unnamed x33, local copies, waits for them, and re-layouts  56.8 us
    reduce_sum x8, other arithmetic, spread(): jnp.sum(lax.all_gather(jnp.where(mine, value, jnp.zeros_like(value)), axi...  25.5 us
    dot_general x2, matrix products, body(): update = jnp.dot(scaled, across.T, precision=lax.Precision.HIGHEST)  21 us
    all_gather x6, local copies, waits for them, and re-layouts, spread(): lax.all_gather(jnp.where(mine, value, jnp.zeros_like(value)), axis)  20.4 us
  transfers between devices with their start and end apart: 8, of which 8 were waited for; matrix products, arithmetic and copies ran while one was open for 3% of the time, Pallas kernels for 0%

profile of v1, /device:TPU:0, one launch (start us, length us, event | category | flops | bytes accessed | tf_op | source)
XLA Modules:
  0.0 855.3 jit_solution(5664902703343524914)
XLA Ops:
  9.5 2.0 fusion.84
  14.2 6.0 copy.23
  20.3 2.9 bitcast_select_fusion.3
  23.2 2.2 copy-done
  25.4 1.8 dynamic-slice_select_fusion
  29.7 98.9 %all-gather.17.cloned.1.call-done = f32[12288,384]{0,1:T(8,128)} async-done(((f32[1536,384]{0,1:T(8,128)}), f32[12288,384]{0,1:T(8,128)}) %all-gather.17.cloned.1.call-update) | async-done | bytes 18874384 | tf_op jit(solution)/shard_map/all_gather | solution.py:11
  128.6 19.6 %copy.30 = f32[48,8,8,1536]{3,2,1,0:T(8,128)S(1)} copy(f32[48,8,8,1536]{3,1,2,0:T(8,128)} %bitcast.136) | data formatting | bytes 37748736
  148.2 4.8 bitcast_reduce_fusion.1
  164.6 41.0 %all-gather.19.cloned.1.call-done = f32[1536,384]{0,1:T(8,128)} async-done(((f32[384,384]{0,1:T(8,128)}), f32[1536,384]{0,1:T(8,128)}) %all-gather.19.cloned.1.call-update) | async-done | bytes 2359312 | tf_op jit(solution)/shard_map/all_gather | solution.py:11
  205.5 3.1 reshape.142
  210.4 11.7 %cholesky.208 = f32[128,128]{1,0:T(8,128)S(1)} custom-call(f32[128,128]{1,0:T(8,128)S(1)} %cholesky.310), custom_call_target="Cholesky" | custom-call | tf_op jit(solution)/shard_map/jit(cholesky)/cholesky | solution.py:66
  222.1 9.8 %custom-call.20 = f32[1,128,128]{1,2,0:T(8,128)S(1)} custom-call(f32[1,128,128]{2,1,0:T(8,128)S(1)} %get-tuple-element.78), custom_call_target="InvertDiagBlocksLowerTriangular" | custom-call | tf_op jit(solution)/shard_map/jit(cholesky)/cholesky | solution.py:66
  232.5 11.7 %cholesky.227 = f32[128,128]{1,0:T(8,128)S(1)} custom-call(f32[128,128]{1,0:T(8,128)S(1)} %cholesky.314), custom_call_target="Cholesky" | custom-call | tf_op jit(solution)/shard_map/jit(cholesky)/cholesky | solution.py:66
  245.6 10.0 %custom-call.21 = f32[1,128,128]{1,2,0:T(8,128)S(1)} custom-call(f32[1,128,128]{2,1,0:T(8,128)S(1)} %get-tuple-element.75), custom_call_target="InvertDiagBlocksLowerTriangular" | custom-call | tf_op jit(solution)/shard_map/jit(cholesky)/cholesky | solution.py:66
  256.1 11.7 %cholesky.246 = f32[128,128]{1,0:T(8,128)S(1)} custom-call(f32[128,128]{1,0:T(8,128)S(1)} %convolution_subtract_fusion.7), custom_call_target="Cholesky" | custom-call | tf_op jit(solution)/shard_map/jit(cholesky)/cholesky | solution.py:66
  270.4 6.1 while.4
  276.5 29.5 %custom-call.22 = f32[3,128,128]{1,2,0:T(8,128)S(1)} custom-call(f32[3,128,128]{2,1,0:T(8,128)S(1)} %get-tuple-element.21), custom_call_target="InvertDiagBlocksLowerTriangular" | custom-call | tf_op jit(solution)/shard_map/jit(_solve_triangular)/triangular_solve | solution.py:67
  307.8 5.7 fusion.6
  325.0 38.8 %all-gather.21.cloned.1.call-done = f32[1536,384]{0,1:T(8,128)} async-done(((f32[384,384]{0,1:T(8,128)}), f32[1536,384]{0,1:T(8,128)}) %all-gather.21.cloned.1.call-update) | async-done | bytes 2359312 | tf_op jit(solution)/shard_map/all_gather | solution.py:11
  363.8 3.7 reshape.143
  367.6 3.1 reduce_sum.200
  370.6 43.4 %all-gather.23.cloned.1.call-done = f32[1536,384]{0,1:T(8,128)} async-done(((f32[384,384]{0,1:T(8,128)}), f32[1536,384]{0,1:T(8,128)}) %all-gather.23.cloned.1.call-update) | async-done | bytes 2359312 | tf_op jit(solution)/shard_map/all_gather | solution.py:11
  414.0 3.5 reshape.144
  417.5 3.9 reduce_sum.202
  421.4 10.6 %fusion.1 = f32[1536,768]{0,1:T(8,128)S(1)} fusion(f32[1536,768]{0,1:T(8,128)} %copy-done, f32[1536,384]{0,1:T(8,128)S(1)} %fusion.6, pred[1536,2]{0,1:T(4,128)(4,1)} %bitcast.143, f32[384,384]{0,1:T(8,128)} %reduce_sum.202, f32[384,384]{0,1:T(8,128)S(1)} %reduce_sum.200), kind=kOutput, calls=%fused_computation.14 | convolution fusion | flops 5438472192 | bytes 12979200 | tf_op jit(solution)/shard_map/dot_general | solution.py:77
  435.3 2.6 fusion.3
  440.2 95.2 %all-gather.25.cloned.1.call-done = f32[12288,384]{0,1:T(8,128)} async-done(((f32[1536,384]{0,1:T(8,128)}), f32[12288,384]{0,1:T(8,128)}) %all-gather.25.cloned.1.call-update) | async-done | bytes 18874384 | tf_op jit(solution)/shard_map/all_gather | solution.py:11
  535.4 20.0 %copy.33 = f32[48,8,8,1536]{3,2,1,0:T(8,128)S(1)} copy(f32[48,8,8,1536]{3,1,2,0:T(8,128)} %bitcast.135) | data formatting | bytes 37748736
  555.4 4.8 bitcast_reduce_fusion
  563.3 49.4 %all-gather.27.cloned.1.call-done = f32[1536,384]{0,1:T(8,128)} async-done(((f32[384,384]{0,1:T(8,128)}), f32[1536,384]{0,1:T(8,128)}) %all-gather.27.cloned.1.call-update) | async-done | bytes 2359312 | tf_op jit(solution)/shard_map/all_gather | solution.py:11
  612.7 2.8 reshape.146
  617.2 11.7 %cholesky.261 = f32[128,128]{1,0:T(8,128)S(1)} custom-call(f32[128,128]{1,0:T(8,128)S(1)} %cholesky.318), custom_call_target="Cholesky" | custom-call | tf_op jit(solution)/shard_map/jit(cholesky)/cholesky | solution.py:66
  629.0 9.8 %custom-call.23 = f32[1,128,128]{1,2,0:T(8,128)S(1)} custom-call(f32[1,128,128]{2,1,0:T(8,128)S(1)} %get-tuple-element.71), custom_call_target="InvertDiagBlocksLowerTriangular" | custom-call | tf_op jit(solution)/shard_map/jit(cholesky)/cholesky | solution.py:66
  639.4 11.7 %cholesky.280 = f32[128,128]{1,0:T(8,128)S(1)} custom-call(f32[128,128]{1,0:T(8,128)S(1)} %cholesky.322), custom_call_target="Cholesky" | custom-call | tf_op jit(solution)/shard_map/jit(cholesky)/cholesky | solution.py:66
  652.5 10.2 %custom-call.24 = f32[1,128,128]{1,2,0:T(8,128)S(1)} custom-call(f32[1,128,128]{2,1,0:T(8,128)S(1)} %get-tuple-element.68), custom_call_target="InvertDiagBlocksLowerTriangular" | custom-call | tf_op jit(solution)/shard_map/jit(cholesky)/cholesky | solution.py:66
  663.2 11.7 %cholesky.299 = f32[128,128]{1,0:T(8,128)S(1)} custom-call(f32[128,128]{1,0:T(8,128)S(1)} %convolution_subtract_fusion.6), custom_call_target="Cholesky" | custom-call | tf_op jit(solution)/shard_map/jit(cholesky)/cholesky | solution.py:66
  677.6 6.1 while.5
  683.8 29.5 %custom-call.25 = f32[3,128,128]{1,2,0:T(8,128)S(1)} custom-call(f32[3,128,128]{2,1,0:T(8,128)S(1)} %get-tuple-element.22), custom_call_target="InvertDiagBlocksLowerTriangular" | custom-call | tf_op jit(solution)/shard_map/jit(_solve_triangular)/triangular_solve | solution.py:67
  715.1 5.7 fusion.4
  726.6 44.6 %all-gather.29.cloned.1.call-done = f32[1536,384]{0,1:T(8,128)} async-done(((f32[384,384]{0,1:T(8,128)}), f32[1536,384]{0,1:T(8,128)}) %all-gather.29.cloned.1.call-update) | async-done | bytes 2359312 | tf_op jit(solution)/shard_map/all_gather | solution.py:11
  771.1 3.7 reshape.147
  774.8 3.1 reduce_sum.206
  777.9 43.6 %all-gather.31.cloned.1.call-done = f32[1536,384]{0,1:T(8,128)} async-done(((f32[384,384]{0,1:T(8,128)}), f32[1536,384]{0,1:T(8,128)}) %all-gather.31.cloned.1.call-update) | async-done | bytes 2359312 | tf_op jit(solution)/shard_map/all_gather | solution.py:11
  821.5 3.5 reshape.148
  825.0 3.1 reduce_sum.207
  828.1 10.4 %fusion = f32[1536,768]{0,1:T(8,128)S(1)} fusion(f32[1536,384]{0,1:T(8,128)} %copy-done.2, f32[1536,384]{0,1:T(8,128)} %copy-done.1, f32[1536,384]{0,1:T(8,128)S(1)} %fusion.4, pred[1536,2]{0,1:T(4,128)(4,1)} %bitcast.144, f32[384,384]{0,1:T(8,128)S(1)} %reduce_sum.207, f32[384,384]{0,1:T(8,128)S(1)} %reduce_sum.206), kind=kOutput, calls=%fused_computation.13 | convolution fusion | flops 5439651840 | bytes 12979200 | tf_op jit(solution)/shard_map/dot_general | solution.py:77
  839.6 2.6 bitcast_select_fusion.2
  842.2 6.0 copy.28
  (144 shorter events, 57.2 us)
Async XLA Ops:
  6.5 122.1 %all-gather.17.cloned.1.call-start = ((), (), s32[]{:S(2)}) async-start(), calls=%async_computation | async-start | bytes 21233664 | tf_op jit(solution)/shard_map/all_gather | solution.py:11
  8.2 12.1 %copy-start.9 = (s32[2]{0:T(128)}, s32[2]{0:T(128)S(1)}, u32[]{:S(2)}) copy-start(s32[2]{0:T(128)S(1)} %fusion.80) | copy-start | bytes 28
  23.2 2.2 copy-start
  27.1 178.4 %all-gather.19.cloned.1.call-start = ((), (), s32[]{:S(2)}) async-start(), calls=%async_computation.1 | async-start | bytes 2949120 | tf_op jit(solution)/shard_map/all_gather | solution.py:11
  148.2 14.1 %copy-start.7 = (s32[16,16]{1,0:T(8,128)S(1)}, s32[16,16]{1,0:T(8,128)}, u32[]{:S(2)}) copy-start(s32[16,16]{1,0:T(8,128)} %param.8) | copy-start | bytes 3076
  153.0 1.4 copy-start.3
  155.4 208.4 %all-gather.21.cloned.1.call-start = ((), (), s32[]{:S(2)}) async-start(), calls=%async_computation.2 | async-start | bytes 2949120 | tf_op jit(solution)/shard_map/all_gather | solution.py:11
  210.3 60.0 %copy-start.11 = (s32[3]{0:T(128)S(1)}, s32[3]{0:T(128)}, u32[]{:S(2)}) copy-start(s32[3]{0:T(128)} %iota_multiply_fusion) | copy-start | bytes 40
  314.9 99.1 %all-gather.23.cloned.1.call-start = ((), (), s32[]{:S(2)}) async-start(), calls=%async_computation.3 | async-start | bytes 2949120 | tf_op jit(solution)/shard_map/all_gather | solution.py:11
  315.5 219.9 %all-gather.25.cloned.1.call-start = ((), (), s32[]{:S(2)}) async-start(), calls=%async_computation.4 | async-start | bytes 21233664 | tf_op jit(solution)/shard_map/all_gather | solution.py:11
  421.4 10.6 %copy-start.6 = (f32[48,8,4,384]{3,1,2,0:T(8,128)S(1)}, f32[48,8,4,384]{3,1,2,0:T(8,128)}, u32[]{:S(2)}) copy-start(f32[48,8,4,384]{3,1,2,0:T(8,128)} %copy.31) | copy-start | bytes 7077892
  433.1 1.4 copy-start.1
  433.1 2.2 copy-start.2
  437.9 174.8 %all-gather.27.cloned.1.call-start = ((), (), s32[]{:S(2)}) async-start(), calls=%async_computation.5 | async-start | bytes 2949120 | tf_op jit(solution)/shard_map/all_gather | solution.py:11
  555.4 7.2 copy-start.10
  560.2 1.4 copy-start.4
  562.6 208.6 %all-gather.29.cloned.1.call-start = ((), (), s32[]{:S(2)}) async-start(), calls=%async_computation.6 | async-start | bytes 2949120 | tf_op jit(solution)/shard_map/all_gather | solution.py:11
  720.8 3.5 copy-start.8
  722.2 99.3 %all-gather.31.cloned.1.call-start = ((), (), s32[]{:S(2)}) async-start(), calls=%async_computation.7 | async-start | bytes 2949120 | tf_op jit(solution)/shard_map/all_gather | solution.py:11
  828.1 10.5 %copy-start.5 = (f32[48,8,4,384]{3,1,2,0:T(8,128)S(1)}, f32[48,8,4,384]{3,1,2,0:T(8,128)}, u32[]{:S(2)}) copy-start(f32[48,8,4,384]{3,1,2,0:T(8,128)} %copy.34) | copy-start | bytes 7077892
Sparse Core Ops, SparseCore 0:
  27.2 101.3 all-gather.16
  155.5 49.9 all-gather.18
  315.0 48.7 all-gather.20
  365.2 48.7 all-gather.22
  438.0 97.3 all-gather.24
  562.7 49.9 all-gather.26
  722.3 48.7 all-gather.28
  772.7 48.7 all-gather.30
